TPU v7x, 256 devices: a whole 4x4x8 slice. The times are simulated.
256 devices in a mesh: panel: 64 (over y, z, core), chan: 4 (over x).
Axes of the slice: x: 4, y: 4, z: 8, core: 2. Of those that a mesh axis runs over, the one named last changes fastest.
Arguments:
- wavefunction: bfloat16 [4, 64, 768, 768], P('chan', 'panel'), may hold values from -6 to 6
- left_env: bfloat16 [2, 64, 768, 768], P(None, 'panel'), may hold values from -0.21875 to 0.21875
- right_env: bfloat16 [2, 64, 768, 768], P(None, 'panel'), may hold values from -0.21875 to 0.21875
- coupling: float32 [2, 4, 4], replicated, may hold values from -4 to 4
- sec_size: int32 [64], replicated, may hold values from 384 to 768, as said below
Outputs:
- applied: bfloat16 [4, 64, 768, 768], P('chan', 'panel')
Inputs may be any that keep to these rules, and one draw needn't show every extreme that they name: `sec_size`: sector sizes; some sector holds exactly 768 states.
All inputs are finite; a program needn't handle non-finite values.
Results may differ from a plain program's by a relative error of at most 0.008.
Values may be sent and summed in bfloat16 or wider, within the bound.
No kernel may reach another device: no remote copies, remote signals or barrier semaphores. Data moves between devices by JAX's collectives and lax.ppermute only.
A program may use at most 128 MiB of HBM per device.

v0:
```python
import jax
import jax.numpy as jnp
from jax import lax
from jax.sharding import PartitionSpec as P

CHARGE_TABLE = (0, 1, 1, 2)


def from_behind(block, axis, distance):
    devices = range(lax.axis_size(axis))
    route = [(i - distance, i) for i in devices if i - distance in devices]
    return lax.ppermute(block, axis, route)


def pick_entry(lookup_table, position):
    slot_ids = jnp.arange(lookup_table.shape[0], dtype=jnp.int32)
    return jnp.sum(jnp.where(slot_ids == position, lookup_table, jnp.zeros_like(lookup_table)))


def pick_column(matrix, position):
    slot_ids = jnp.arange(matrix.shape[1], dtype=jnp.int32)
    return jnp.sum(jnp.where(slot_ids[None, :] == position, matrix, 0.0), axis=1)


def outer_dot(left_matrix, right_matrix):
    return lax.dot_general(
        left_matrix, right_matrix, (((1,), (1,)), ((), ())), preferred_element_type=jnp.float32
    )


def coupling_masks(coupling):
    charges = jnp.array(CHARGE_TABLE, jnp.int32)
    same_charge = charges[:, None] == charges[None, :]
    raised_charge = charges[None, :] == charges[:, None] + 1
    return (jnp.where(same_charge, coupling[0], 0.0), jnp.where(raised_charge, coupling[1], 0.0))


def block_mask(sec_size, sector, charge, sector_width):
    sector_count = sec_size.shape[0]
    target = sector + charge
    exists = target < sector_count
    rows_live = pick_entry(sec_size, sector)
    cols_live = pick_entry(sec_size, target)
    positions = jnp.arange(sector_width, dtype=jnp.int32)
    row_ok = positions[:, None] < rows_live
    col_ok = positions[None, :] < cols_live
    return jnp.logical_and(jnp.logical_and(row_ok, col_ok), exists)


def choose_block(charge, own_block, near_block, far_block):
    return jnp.where(charge == 0, own_block, jnp.where(charge == 1, near_block, far_block))


def shards(wavefunction, left_env, right_env, coupling, sec_size):
    sector_width = wavefunction.shape[-1]
    pair_index = lax.axis_index("chan")
    sector = lax.axis_index("panel")
    charge = pick_entry(jnp.array(CHARGE_TABLE, jnp.int32), pair_index)
    keep_mask = block_mask(sec_size, sector, charge, sector_width)
    masked = jnp.where(keep_mask, wavefunction[0, 0], jnp.zeros((), jnp.bfloat16))
    same_coef, raise_coef = coupling_masks(coupling)
    near_right = from_behind(right_env, "panel", -1)
    far_right = from_behind(right_env, "panel", -2)
    right_here = choose_block(charge, right_env[:, 0], near_right[:, 0], far_right[:, 0])
    lower = from_behind(masked, "panel", 1)
    pair_here, pair_lower = (
        lax.all_gather(masked[None], "chan", axis=0, tiled=True),
        lax.all_gather(lower[None], "chan", axis=0, tiled=True),
    )
    plan_tables = (
        ((0, 0, 0, 0), (0, 1, 2, 3), (1, 1, 1, 1)),
        ((1, 0, 0, 0), (2, 2, 1, 3), (1, 1, 1, 0)),
        ((1, 1, 1, 1), (1, 3, 3, 3), (1, 1, 1, 1)),
    )
    summed_total = jnp.zeros((sector_width, sector_width), jnp.float32)
    for channel_table, partner_table, flag_table in plan_tables:
        channel = pick_entry(jnp.array(channel_table, jnp.int32), pair_index)
        partner = pick_entry(jnp.array(partner_table, jnp.int32), pair_index)
        active = pick_entry(jnp.array(flag_table, jnp.int32), pair_index)
        source = jnp.where(channel == 0, pair_here, pair_lower)
        coef_matrix = jnp.where(channel == 0, same_coef, raise_coef)
        panel_block = lax.dynamic_index_in_dim(source, partner, 0, keepdims=False)
        left_block = lax.dynamic_index_in_dim(left_env[:, 0], channel, 0, keepdims=False)
        right_block = lax.dynamic_index_in_dim(right_here, channel, 0, keepdims=False)
        weight = pick_entry(
            pick_column(jnp.transpose(coef_matrix), pair_index), partner
        ) * active.astype(jnp.float32)
        product = jnp.dot(left_block, panel_block, preferred_element_type=jnp.float32).astype(
            jnp.bfloat16
        )
        summed_total = summed_total + weight * outer_dot(product, right_block)
    applied = jnp.where(keep_mask, summed_total, 0.0).astype(jnp.bfloat16)
    return applied[None, None]


def solution(mesh):
    return jax.shard_map(
        shards,
        mesh=mesh,
        in_specs=(
            P("chan", "panel", None, None),
            P(None, "panel", None, None),
            P(None, "panel", None, None),
            P(),
            P(),
        ),
        out_specs=P("chan", "panel", None, None),
        check_vma=False,
    )
```

profile of v0, /device:TPU:1, one launch (start us, length us, event | category | flops | bytes accessed | tf_op | source)
XLA Modules:
  0.0 149.6 jit_solution(13961359001987056313)
XLA Ops:
  6.5 0.0 copy-start
  6.5 0.0 all-gather.4.cloned.1.call-start
  6.5 1.4 select_reduce_fusion.9
  8.6 1.4 fusion.42
  10.0 1.3 iota_compare_fusion
  11.3 2.8 %and_select_fusion = bf16[1,768,768]{2,1,0:T(8,128)(2,1)} fusion(bf16[1,1,768,768]{3,2,1,0:T(8,128)(2,1)} %param.16, pred[]{:T(512)S(6)} %lt.52, pred[768]{0:T(1024)(128)(4,1)S(1)} %get-tuple-element.14, pred[768]{0:T(1024)(128)(4,1)S(1)} %get-tuple-element.15), kind=kLoop, calls=%fused_computation.2 | loop fusion | flops 1769472 | bytes 2360833 | tf_op jit(solution)/shard_map/jit(_where)/select_n | solution.py:60
  14.1 0.0 copy-start.1
  14.1 0.0 copy-start.4
  14.1 0.0 copy-start.5
  14.1 0.0 all-gather.4.cloned.1.call-update
  14.2 0.0 all-gather.6.cloned.1.call-start
  14.2 0.0 copy-done
  14.2 0.5 fusion
  14.7 5.1 %collective-permute-start = (bf16[768,768]{1,0:T(8,128)(2,1)S(1)}, bf16[768,768]{1,0:T(8,128)(2,1)S(1)}, u32[]{:S(2)}, u32[]{:S(2)}) collective-permute-start(bf16[768,768]{1,0:T(8,128)(2,1)S(1)} %fusion), channel_id=1, source_target_pairs={{0,4},{4,8},{8,12},{12,16},{16,20},{20,24},{24,28},{28,32},{32,36}... | collective-permute-start | bytes 3538952 | tf_op jit(solution)/shard_map/ppermute | solution.py:12
  19.8 13.1 %collective-permute-done = bf16[768,768]{1,0:T(8,128)(2,1)S(1)} collective-permute-done((bf16[768,768]{1,0:T(8,128)(2,1)S(1)}, bf16[768,768]{1,0:T(8,128)(2,1)S(1)}, u32[]{:S(2)}, u32[]{:S(2)}) %collective-permute-start) | collective-permute-done | bytes 1179680 | tf_op jit(solution)/shard_map/ppermute | solution.py:12
  32.9 0.0 copy-start.3
  32.9 1.0 copy-done.3
  33.9 0.0 all-gather.6.cloned.1.call-update
  33.9 0.0 copy-done.1
  33.9 1.9 %collective-permute-start.1 = (bf16[2,1,768,768]{3,2,1,0:T(8,128)(2,1)S(1)}, bf16[2,1,768,768]{3,2,1,0:T(8,128)(2,1)}, u32[]{:S(2)}, u32[]{:S(2)}) collective-permute-start(bf16[2,1,768,768]{3,2,1,0:T(8,128)(2,1)S(1)} %copy-done.1), channel_id=1, source_target_pairs={{4,0},{8,4},{12,8},{16,12},{20,16},{24,20},{28,24},{32,28},{36,32}... | collective-permute-start | bytes 7077896 | tf_op jit(solution)/shard_map/ppermute | solution.py:12
  35.9 1.3 collective-permute-start.2
  37.8 1.4 select_reduce_fusion.3
  40.3 0.6 select_reduce_fusion.8
  43.9 1.3 select_reduce_fusion.6
  49.6 1.3 select_reduce_fusion.4
  51.6 0.0 copy-done.4
  51.6 0.0 copy-done.5
  51.6 0.7 select_reduce_fusion.1
  52.4 1.2 fusion.44
  54.2 1.2 fusion.46
  59.1 1.2 fusion.45
  61.0 27.5 %collective-permute-done.1 = bf16[2,1,768,768]{3,2,1,0:T(8,128)(2,1)} collective-permute-done((bf16[2,1,768,768]{3,2,1,0:T(8,128)(2,1)S(1)}, bf16[2,1,768,768]{3,2,1,0:T(8,128)(2,1)}, u32[]{:S(2)}, u32[]{:S(2)}) %collective-permute-start.1) | collective-permute-done | bytes 2359328 | tf_op jit(solution)/shard_map/ppermute | solution.py:12
  88.5 3.8 %collective-permute-done.2 = bf16[2,1,768,768]{3,2,1,0:T(8,128)(2,1)} collective-permute-done((bf16[2,1,768,768]{3,2,1,0:T(8,128)(2,1)S(1)}, bf16[2,1,768,768]{3,2,1,0:T(8,128)(2,1)}, u32[]{:S(2)}, u32[]{:S(2)}) %collective-permute-start.2) | collective-permute-done | bytes 2359328 | tf_op jit(solution)/shard_map/ppermute | solution.py:12
  92.3 3.7 %select_select_fusion = bf16[2,1,768,768]{3,2,1,0:T(8,128)(2,1)} fusion(bf16[2,1,768,768]{3,2,1,0:T(8,128)(2,1)S(1)} %copy-done.1, bf16[2,1,768,768]{3,2,1,0:T(8,128)(2,1)} %collective-permute-done.1, bf16[2,1,768,768]{3,2,1,0:T(8,128)(2,1)} %collective-permute-done.2, pred[]{:T(512)S(6)} %eq.122, pred[]{:T(512)S(6)} %eq.121), kind=kLoop, calls=%fused_computation.1 | loop fusion | flops 2359296 | bytes 9437186 | tf_op jit(solution)/shard_map/jit(_where)/select_n | solution.py:51
  95.9 0.0 copy-start.2
  95.9 0.0 all-gather.4.cloned.1.call-done
  95.9 6.2 %fusion.8 = f32[768,768]{1,0:T(8,128)} fusion(bf16[2,1,768,768]{3,2,1,0:T(8,128)(2,1)} %select_select_fusion, bf16[2,1,768,768]{3,2,1,0:T(8,128)(2,1)} %param.17, bf16[4,768,768]{2,1,0:T(8,128)(2,1)} %all-gather.4.cloned.1.call-done, s32[]{:T(128)S(6)} %select_n.181), kind=kOutput, calls=%fused_computation.16 | convolution fusion | flops 1812529152 | bytes 5898244 | tf_op jit(solution)/shard_map/dot_general | solution.py:26
  102.2 28.2 %all-gather.6.cloned.1.call-done = bf16[3072,768]{1,0:T(8,128)(2,1)} async-done(((bf16[768,768]{1,0:T(8,128)(2,1)}), bf16[3072,768]{1,0:T(8,128)(2,1)}) %all-gather.6.cloned.1.call-update) | async-done | bytes 4718608 | tf_op jit(solution)/shard_map/all_gather | solution.py:68
  130.4 0.0 copy-done.2
  130.4 5.6 %fusion.11 = f32[768,768]{1,0:T(8,128)} fusion(bf16[2,1,768,768]{3,2,1,0:T(8,128)(2,1)S(1)} %copy-done.2, s32[]{:T(128)S(6)} %select_n.193, bf16[4,768,768]{2,1,0:T(8,128)(2,1)} %bitcast.60, s32[]{:T(128)S(6)} %select_n.196, bf16[4,768,768]{2,1,0:T(8,128)(2,1)} %all-gather.4.cloned.1.call-done, bf16[2,1,768,768]{3,2,1,0:T(8,128)(2,1)} %param.17, pred[]{:T(512)S(6)} %eq.125), kind=kOutput, calls=%fused_computation.19 | convolution fusion | flops 1813118976 | bytes 7079936 | tf_op jit(solution)/shard_map/dot_general | solution.py:26
  136.0 6.8 %fusion.1 = bf16[1,1,768,768]{3,2,1,0:T(8,128)(2,1)} fusion(f32[768,768]{1,0:T(8,128)} %fusion.11, f32[768,768]{1,0:T(8,128)} %fusion.8, bf16[2,1,768,768]{3,2,1,0:T(8,128)(2,1)S(1)} %copy-done.2, s32[]{:T(128)S(6)} %select_n.204, f32[]{:T(128)S(6)} %mul.33, f32[]{:T(128)S(6)} %mul.30, f32[]{:T(128)S(6)} %mul.27, pred[]{:T(512)S(6)} %lt.52, ...), kind=kOutput, calls=%fused_computation.8 | convolution fusion | flops 1818427392 | bytes 10622976 | tf_op jit(solution)/shard_map/dot_general | solution.py:26
  (1 shorter events, 0.0 us)
Async XLA Ops:
  6.5 7.7 %copy-start = (bf16[1,1,768,768]{3,2,1,0:T(8,128)(2,1)S(1)}, bf16[1,1,768,768]{3,2,1,0:T(8,128)(2,1)}, u32[]{:S(2)}) copy-start(bf16[1,1,768,768]{3,2,1,0:T(8,128)(2,1)} %param.16) | copy-start | bytes 3538948
  6.5 89.4 %all-gather.4.cloned.1.call-start = ((), (), s32[]{:S(2)}) async-start(), calls=%async_computation | async-start | bytes 5898240 | tf_op jit(solution)/shard_map/all_gather | solution.py:67
  14.1 19.8 %copy-start.1 = (bf16[2,1,768,768]{3,2,1,0:T(8,128)(2,1)S(1)}, bf16[2,1,768,768]{3,2,1,0:T(8,128)(2,1)}, u32[]{:S(2)}) copy-start(bf16[2,1,768,768]{3,2,1,0:T(8,128)(2,1)} %param.18) | copy-start | bytes 7077892
  14.1 37.5 %copy-start.4 = (f32[2,4,4]{2,1,0:T(4,128)S(1)}, f32[2,4,4]{2,1,0:T(4,128)}, u32[]{:S(2)}) copy-start(f32[2,4,4]{2,1,0:T(4,128)} %param.19) | copy-start | bytes 388
  14.1 37.5 %copy-start.5 = (s32[4]{0:T(128)S(1)}, s32[4]{0:T(128)}, u32[]{:S(2)}) copy-start(s32[4]{0:T(128)} %constant.69.clone) | copy-start | bytes 52
  14.2 116.2 %all-gather.6.cloned.1.call-start = ((), (), s32[]{:S(2)}) async-start(), calls=%async_computation.1 | async-start | bytes 5898240 | tf_op jit(solution)/shard_map/all_gather | solution.py:68
  14.7 18.2 %collective-permute-start = (bf16[768,768]{1,0:T(8,128)(2,1)S(1)}, bf16[768,768]{1,0:T(8,128)(2,1)S(1)}, u32[]{:S(2)}, u32[]{:S(2)}) collective-permute-start(bf16[768,768]{1,0:T(8,128)(2,1)S(1)} %fusion), channel_id=1, source_target_pairs={{0,4},{4,8},{8,12},{12,16},{16,20},{20,24},{24,28},{28,32},{32,36}... | collective-permute-start | bytes 3538952 | tf_op jit(solution)/shard_map/ppermute | solution.py:12
  32.9 1.0 copy-start.3
  33.9 54.6 %collective-permute-start.1 = (bf16[2,1,768,768]{3,2,1,0:T(8,128)(2,1)S(1)}, bf16[2,1,768,768]{3,2,1,0:T(8,128)(2,1)}, u32[]{:S(2)}, u32[]{:S(2)}) collective-permute-start(bf16[2,1,768,768]{3,2,1,0:T(8,128)(2,1)S(1)} %copy-done.1), channel_id=1, source_target_pairs={{4,0},{8,4},{12,8},{16,12},{20,16},{24,20},{28,24},{32,28},{36,32}... | collective-permute-start | bytes 7077896 | tf_op jit(solution)/shard_map/ppermute | solution.py:12
  35.9 56.4 %collective-permute-start.2 = (bf16[2,1,768,768]{3,2,1,0:T(8,128)(2,1)S(1)}, bf16[2,1,768,768]{3,2,1,0:T(8,128)(2,1)}, u32[]{:S(2)}, u32[]{:S(2)}) collective-permute-start(bf16[2,1,768,768]{3,2,1,0:T(8,128)(2,1)S(1)} %copy-done.1), channel_id=1, source_target_pairs={{8,0},{12,4},{16,8},{20,12},{24,16},{28,20},{32,24},{36,28},{40,32... | collective-permute-start | bytes 7077896 | tf_op jit(solution)/shard_map/ppermute | solution.py:12
  95.9 34.5 %copy-start.2 = (bf16[2,1,768,768]{3,2,1,0:T(8,128)(2,1)S(1)}, bf16[2,1,768,768]{3,2,1,0:T(8,128)(2,1)}, u32[]{:S(2)}) copy-start(bf16[2,1,768,768]{3,2,1,0:T(8,128)(2,1)} %select_select_fusion) | copy-start | bytes 7077892
Sparse Core Ops, SparseCore 0:
  14.3 58.6 all-gather.3
  74.8 55.5 all-gather.5
where the time goes:
time: 150 us
  waiting for transfers between devices  72.7 us (48%)
  between operations  28.8 us (19%)
  other arithmetic  20.2 us (13%)
  matrix products  18.6 us (12%)
  starting transfers between devices  8.31 us (6%)
    ppermute x3, waiting for transfers between devices, from_behind(): return lax.ppermute(block, axis, route)  44.4 us
    all_gather x1, waiting for transfers between devices, shards(): lax.all_gather(lower[None], 'chan', axis=0, tiled=True)  28.2 us
    dot_general x3, matrix products, outer_dot(): lax.dot_general(left_matrix, right_matrix, (((1,), (1,)), ((), ())), pref...  18.6 us
    reduce_sum x9, other arithmetic, pick_entry(): jnp.sum(jnp.where(slot_ids == position, lookup_table, jnp.zeros_like(look...  11.2 us
    ppermute x3, starting transfers between devices, from_behind(): return lax.ppermute(block, axis, route)  8.27 us
    select_n x1, other arithmetic, choose_block(): jnp.where(charge == 0, own_block, jnp.where(charge == 1, near_block, far_...  3.67 us
    select_n x2, other arithmetic, shards(): jnp.where(keep_mask, wavefunction[0, 0], jnp.zeros((), jnp.bfloat16))  3.29 us
  transfers between devices with their start and end apart: 5, of which 4 were waited for; matrix products, arithmetic and copies ran while one was open for 13% of the time, Pallas kernels for 0%

commit v1 on v0

v1 whole, which is shorter than its diff:
```python
import jax
import jax.numpy as jnp
from jax import lax
from jax.experimental import pallas as pl
from jax.experimental.pallas import tpu as pltpu
from jax.sharding import PartitionSpec as P


WIDTHS = (256, 256, 256)
STARTS = tuple(sum(WIDTHS[:i]) for i in range(len(WIDTHS)))
LATE = 1
TILE = 256
AXES = ("panel", "chan")
VMEM_BYTES = 24 * 1024 * 1024


def move(block, sectors, routes):
    pairs = lax.axis_size("chan")
    hops = []
    for source, target, shift in routes:
        for a in range(sectors):
            if 0 <= a + shift < sectors:
                hops.append((a * pairs + source, (a + shift) * pairs + target))
    return lax.ppermute(block, AXES, hops)


def outer_dot(left_matrix, right_matrix):
    return lax.dot_general(
        left_matrix, right_matrix, (((1,), (1,)), ((), ())), preferred_element_type=jnp.float32
    )


def live(sizes, sector):
    count = sizes.shape[0]
    inside = jnp.logical_and(sector >= 0, sector < count)
    return jnp.where(inside, sizes[jnp.clip(sector, 0, count - 1)], 0)


def charge_of(pair):
    return jnp.where(pair == 0, 0, jnp.where(pair == 3, 2, 1))


def inside(rows, cols, first_row, first_col, shape):
    row = first_row + lax.broadcasted_iota(jnp.int32, shape, 0)
    col = first_col + lax.broadcasted_iota(jnp.int32, shape, 1)
    return jnp.logical_and(row < rows, col < cols)


def gate(sizes, pair, sector):
    cols = live(sizes, sector + charge_of(pair))
    return live(sizes, sector), cols, live(sizes, sector - 1)


def kept_kernel(early, coupling, sizes, *refs):
    count = len(WIDTHS)
    own, left, right, following, upper, *rest = refs
    partner, rest = rest[:count], rest[count:]
    relayed, rest = rest[:early], rest[early:]
    acc, mixed, lower = rest
    width = mixed.shape[0]
    pair = lax.axis_index("chan")
    sector = lax.axis_index("panel")
    middle = jnp.logical_or(pair == 1, pair == 2)
    rows, cols, lower_rows = gate(sizes, pair, sector)
    alpha = coupling[0, pair, pair]
    beta = jnp.where(middle, coupling[0, pair, jnp.where(middle, 3 - pair, 0)], 0.0)

    def mix(with_partner):
        for i in range(count):
            at, wide = STARTS[i], WIDTHS[i]
            value = alpha * own[0, 0, :, at : at + wide].astype(jnp.float32)
            if with_partner:
                value = value + beta * partner[i][...].astype(jnp.float32)
            keep = inside(rows, cols, 0, at, value.shape)
            mixed[:, at : at + wide] = jnp.where(keep, value, 0.0).astype(jnp.bfloat16)

    pl.when(middle)(lambda: mix(True))
    pl.when(jnp.logical_not(middle))(lambda: mix(False))

    def kept(target):
        for at in range(0, width, TILE):
            window = pl.ds(at, TILE)
            half = jnp.dot(left[0, 0, window], mixed[...], preferred_element_type=jnp.float32)
            acc[window] = outer_dot(half.astype(jnp.bfloat16), target)

    pl.when(pair == 0)(lambda: kept(right[0, 0]))
    pl.when(pair != 0)(lambda: kept(following[...]))

    if early:
        columns = STARTS[early]
        gamma = jnp.where(pair == 0, 1.0, coupling[1, pair, 3])

        def moved(target):
            for i in range(early):
                at, wide = STARTS[i], WIDTHS[i]
                part = relayed[i][...]
                keep = inside(lower_rows, cols, 0, at, part.shape)
                lower[:, at : at + wide] = jnp.where(keep, part, jnp.zeros_like(part))
            for at in range(0, width, TILE):
                window = pl.ds(at, TILE)
                half = jnp.dot(left[1, 0, window], lower[...], preferred_element_type=jnp.float32)
                half = (gamma * half).astype(jnp.bfloat16)
                acc[window] = acc[window] + outer_dot(half, target)

        pl.when(pair == 0)(lambda: moved(right[1, 0, :, 0:columns]))
        pl.when(jnp.logical_or(pair == 1, pair == 2))(lambda: moved(upper[:, 0:columns]))


def moved_kernel(early, coupling, sizes, *refs):
    count = len(WIDTHS)
    base = STARTS[early]
    acc, left, right, upper, *rest = refs
    relayed, rest = rest[: count - early], rest[count - early :]
    out_ref, lower, out, sems = rest
    width = acc.shape[0]
    pair = lax.axis_index("chan")
    sector = lax.axis_index("panel")
    rows, cols, lower_rows = gate(sizes, pair, sector)

    def store(at, value):
        keep = inside(rows, cols, at, 0, value.shape)
        out[pl.ds(at, TILE)] = jnp.where(keep, value, 0.0).astype(jnp.bfloat16)
        send(at).start()

    def send(at):
        window = pl.ds(at, TILE)
        return pltpu.make_async_copy(out.at[window], out_ref.at[0, 0, window], sems.at[at // TILE])

    @pl.when(pair == 3)
    def _():
        for at in range(0, width, TILE):
            store(at, acc[pl.ds(at, TILE)])

    @pl.when(pair != 3)
    def _():
        for i in range(early, count):
            at, wide = STARTS[i], WIDTHS[i]
            part = relayed[i - early][...]
            keep = inside(lower_rows, cols, 0, at, part.shape)
            lower[:, at - base : at - base + wide] = jnp.where(keep, part, jnp.zeros_like(part))

    def moved(target):
        gamma = jnp.where(pair == 0, 1.0, coupling[1, pair, 3])
        for at in range(0, width, TILE):
            window = pl.ds(at, TILE)
            half = jnp.dot(left[1, 0, window], lower[...], preferred_element_type=jnp.float32)
            term = outer_dot((gamma * half).astype(jnp.bfloat16), target)
            store(at, acc[window] + term)

    pl.when(pair == 0)(lambda: moved(right[1, 0, :, base:width]))
    pl.when(jnp.logical_or(pair == 1, pair == 2))(lambda: moved(upper[:, base:width]))
    for at in range(0, width, TILE):
        send(at).wait()


def cut_kernel(blocks, count, *refs):
    sources, rest = refs[:count], refs[count:]
    targets, sems = rest[len(rest) - 1 - len(blocks) : -1], rest[-1]
    copies = []
    for i, (source, channel, at, wide) in enumerate(blocks):
        part = sources[source].at[channel, 0, :, pl.ds(at, wide)]
        copies.append(pltpu.make_async_copy(part, targets[i], sems.at[i]))
    for copy in copies:
        copy.start()
    for copy in copies:
        copy.wait()


def cut(sources, blocks, *after):
    height = sources[0].shape[-2]
    anywhere = pl.BlockSpec(memory_space=pl.ANY)
    shapes = [jax.ShapeDtypeStruct((height, wide), jnp.bfloat16) for *_, wide in blocks]
    return list(
        pl.pallas_call(
            lambda *refs: cut_kernel(blocks, len(sources), *refs),
            out_shape=shapes,
            in_specs=[anywhere] * (len(sources) + len(after)),
            out_specs=[pl.BlockSpec(memory_space=pltpu.VMEM)] * len(blocks),
            scratch_shapes=[pltpu.SemaphoreType.DMA((len(blocks),))],
            cost_estimate=pl.CostEstimate(
                flops=0, bytes_accessed=4 * height * sum(b[-1] for b in blocks), transcendentals=0
            ),
            compiler_params=pltpu.CompilerParams(vmem_limit_bytes=8 * 1024 * 1024),
        )(*sources, *after)
    )


def raise_kernel(coupling, own, partner, out):
    pair = lax.axis_index("chan")

    @pl.when(pair == 1)
    def _():
        mine = coupling[1, 0, 1] * own[...].astype(jnp.float32)
        theirs = coupling[1, 0, 2] * partner[...].astype(jnp.float32)
        out[...] = (mine + theirs).astype(jnp.bfloat16)

    @pl.when(pair == 0)
    def _():
        out[...] = partner[...]

    @pl.when(pair == 3)
    def _():
        out[...] = own[...]


def raise_part(coupling, own, partner):
    on_chip = pl.BlockSpec(memory_space=pltpu.VMEM)
    return pl.pallas_call(
        raise_kernel,
        out_shape=jax.ShapeDtypeStruct(own.shape, own.dtype),
        in_specs=[pl.BlockSpec(memory_space=pltpu.SMEM), on_chip, on_chip],
        out_specs=on_chip,
        cost_estimate=pl.CostEstimate(flops=3 * own.size, bytes_accessed=6 * own.size, transcendentals=0),
        compiler_params=pltpu.CompilerParams(vmem_limit_bytes=8 * 1024 * 1024),
        name="raise",
    )(coupling, own, partner)


def shards(wavefunction, left_env, right_env, coupling, sec_size):
    width = wavefunction.shape[-1]
    sectors = sec_size.shape[0]
    count = len(WIDTHS)
    early = count - LATE
    blocks = [(0, 0, at, wide) for at, wide in zip(STARTS, WIDTHS)]
    own_part = cut((wavefunction,), blocks[:1])
    cut_later = cut((wavefunction, right_env), blocks[1:] + [(1, 0, 0, width), (1, 1, 0, width)], own_part[0])
    own_part, right_part = own_part + cut_later[: count - 1], cut_later[count - 1 :]
    exchange = ((1, 2, 0), (2, 1, 0), (3, 0, 0))
    partner = [move(part, sectors, exchange) for part in own_part]
    nearby = ((1, 1, -1), (2, 2, -1))
    following = move(right_part[0], sectors, nearby + ((3, 3, -2),))
    upper = move(right_part[1], sectors, nearby)
    onward = ((1, 0, 1), (0, 1, 1), (3, 2, 1))
    relayed = []
    for a, b in zip(own_part, partner):
        value = raise_part(coupling, a, b)
        relayed.append(move(value, sectors, onward))

    scalars = pl.BlockSpec(memory_space=pltpu.SMEM)
    on_chip = pl.BlockSpec(memory_space=pltpu.VMEM)
    acc = pl.pallas_call(
        lambda *refs: kept_kernel(early, *refs),
        out_shape=jax.ShapeDtypeStruct((width, width), jnp.float32),
        in_specs=[scalars] * 2 + [on_chip] * (5 + count + early),
        out_specs=on_chip,
        scratch_shapes=[
            pltpu.VMEM((width, width), jnp.bfloat16),
            pltpu.VMEM((width, STARTS[early] if early else 128), jnp.bfloat16),
        ],
        cost_estimate=pl.CostEstimate(
            flops=8 * width**3, bytes_accessed=18 * width * width, transcendentals=0
        ),
        compiler_params=pltpu.CompilerParams(vmem_limit_bytes=VMEM_BYTES),
        name="kept",
    )(coupling, sec_size, wavefunction, left_env, right_env, following, upper, *partner, *relayed[:early])
    columns = width - STARTS[early]
    out = pl.pallas_call(
        lambda *refs: moved_kernel(early, *refs),
        out_shape=jax.ShapeDtypeStruct((1, 1, width, width), jnp.bfloat16),
        in_specs=[scalars] * 2 + [on_chip] * (4 + LATE),
        out_specs=pl.BlockSpec(memory_space=pl.ANY),
        scratch_shapes=[
            pltpu.VMEM((width, columns), jnp.bfloat16),
            pltpu.VMEM((width, width), jnp.bfloat16),
            pltpu.SemaphoreType.DMA((width // TILE,)),
        ],
        cost_estimate=pl.CostEstimate(
            flops=4 * width * width * columns, bytes_accessed=10 * width * width, transcendentals=0
        ),
        compiler_params=pltpu.CompilerParams(vmem_limit_bytes=VMEM_BYTES),
        name="moved",
    )(coupling, sec_size, acc, left_env, right_env, upper, *relayed[early:])
    return out


def solution(mesh):
    return jax.shard_map(
        shards,
        mesh=mesh,
        in_specs=(
            P("chan", "panel", None, None),
            P(None, "panel", None, None),
            P(None, "panel", None, None),
            P(),
            P(),
        ),
        out_specs=P("chan", "panel", None, None),
        check_vma=False,
    )
```

time: 150 us -> 61.3 us (0.41)
  the two profiles are of different devices: /device:TPU:1 before, /device:TPU:9 now
where the time goes in v1:
time: 61.3 us; the launch traced here: 61 us
  waiting for transfers between devices  34.8 us (57%)
  starting transfers between devices  13 us (21%)
  Pallas kernels  10.1 us (16%)
  local copies, waits for them, and re-layouts  2.95 us (5%)
    ppermute x8, waiting for transfers between devices, move(): return lax.ppermute(block, AXES, hops)  34.8 us
    ppermute x8, starting transfers between devices, move(): return lax.ppermute(block, AXES, hops)  13 us
    pallas_call x1, Pallas kernels, shards(): pl.pallas_call(lambda *refs: kept_kernel(early, *refs), out_shape=jax.Sha...  4.97 us
    unnamed x14, local copies, waits for them, and re-layouts  2.95 us
    pallas_call x1, Pallas kernels, shards(): pl.pallas_call(lambda *refs: moved_kernel(early, *refs), out_shape=jax.Sh...  2.57 us
    pallas_call x3, Pallas kernels, raise_part(): pl.pallas_call(raise_kernel, out_shape=jax.ShapeDtypeStruct(own.shape, ow...  1.93 us
  transfers between devices with their start and end apart: 8, of which 5 were waited for; matrix products, arithmetic and copies ran while one was open for 0% of the time, Pallas kernels for 11%

profile of v1, /device:TPU:9, one launch (start us, length us, event | category | flops | bytes accessed | tf_op | source)
XLA Modules:
  0.0 61.0 jit_solution(9722000107796494035)
XLA Ops:
  0.0 0.0 copy-start.2
  0.0 1.3 %copy-done.2 = bf16[1,1,768,768]{3,2,1,0:T(8,128)(2,1)S(1)} copy-done((bf16[1,1,768,768]{3,2,1,0:T(8,128)(2,1)S(1)}, bf16[1,1,768,768]{3,2,1,0:T(8,128)(2,1)}, u32[]{:S(2)}) %copy-start.2) | copy-done | bytes 1179672
  1.3 0.0 copy-start
  1.3 1.7 %copy-done = bf16[2,1,768,768]{3,2,1,0:T(8,128)(2,1)S(1)} copy-done((bf16[2,1,768,768]{3,2,1,0:T(8,128)(2,1)S(1)}, bf16[2,1,768,768]{3,2,1,0:T(8,128)(2,1)}, u32[]{:S(2)}) %copy-start) | copy-done | bytes 2359320
  3.0 0.0 copy-start.5
  3.0 0.0 copy-start.4
  3.0 0.6 shard_map.56
  3.6 0.9 %collective-permute-start = (bf16[768,768]{1,0:T(8,128)(2,1)S(1)}, bf16[768,768]{1,0:T(8,128)(2,1)S(1)}, u32[]{:S(2)}, u32[]{:S(2)}) collective-permute-start(bf16[768,768]{1,0:T(8,128)(2,1)S(1)} %get-tuple-element.9), channel_id=1, source_target_pairs={{5,1},{9,5},{13,9},{17,13},{21,17},{25,21},{29,25},{33,29},{37,33}... | collective-permute-start | bytes 3538952 | tf_op jit(solution)/shard_map/ppermute | solution.py:24
  4.4 0.7 %collective-permute-start.1 = (bf16[768,768]{1,0:T(8,128)(2,1)S(1)}, bf16[768,768]{1,0:T(8,128)(2,1)S(1)}, u32[]{:S(2)}, u32[]{:S(2)}) collective-permute-start(bf16[768,768]{1,0:T(8,128)(2,1)S(1)} %get-tuple-element.10), channel_id=1, source_target_pairs={{5,1},{9,5},{13,9},{17,13},{21,17},{25,21},{29,25},{33,29},{37,33}... | collective-permute-start | bytes 3538952 | tf_op jit(solution)/shard_map/ppermute | solution.py:24
  5.2 1.3 %collective-permute-start.2 = (bf16[768,256]{1,0:T(8,128)(2,1)S(1)}, bf16[768,256]{1,0:T(8,128)(2,1)S(1)}, u32[]{:S(2)}, u32[]{:S(2)}) collective-permute-start(bf16[768,256]{1,0:T(8,128)(2,1)S(1)} %shard_map.55.refs_2_.own), channel_id=1, source_target_pairs={{1,2},{5,6},{9,10},{13,14},{17,18},{21,22},{25,26},{29,30},{33,34}... | collective-permute-start | bytes 1179656 | tf_op jit(solution)/shard_map/ppermute | solution.py:24
  6.5 1.3 %collective-permute-start.3 = (bf16[768,256]{1,0:T(8,128)(2,1)S(1)}, bf16[768,256]{1,0:T(8,128)(2,1)S(1)}, u32[]{:S(2)}, u32[]{:S(2)}) collective-permute-start(bf16[768,256]{1,0:T(8,128)(2,1)S(1)} %get-tuple-element.11.own), channel_id=1, source_target_pairs={{1,2},{5,6},{9,10},{13,14},{17,18},{21,22},{25,26},{29,30},{33,34}... | collective-permute-start | bytes 1179656 | tf_op jit(solution)/shard_map/ppermute | solution.py:24
  7.8 1.3 %collective-permute-start.4 = (bf16[768,256]{1,0:T(8,128)(2,1)S(1)}, bf16[768,256]{1,0:T(8,128)(2,1)S(1)}, u32[]{:S(2)}, u32[]{:S(2)}) collective-permute-start(bf16[768,256]{1,0:T(8,128)(2,1)S(1)} %get-tuple-element.12.own), channel_id=1, source_target_pairs={{1,2},{5,6},{9,10},{13,14},{17,18},{21,22},{25,26},{29,30},{33,34}... | collective-permute-start | bytes 1179656 | tf_op jit(solution)/shard_map/ppermute | solution.py:24
  9.1 15.0 %collective-permute-done.2.partner.refs_7_ = bf16[768,256]{1,0:T(8,128)(2,1)S(1)} collective-permute-done((bf16[768,256]{1,0:T(8,128)(2,1)S(1)}, bf16[768,256]{1,0:T(8,128)(2,1)S(1)}, u32[]{:S(2)}, u32[]{:S(2)}) %collective-permute-start.2) | collective-permute-done | bytes 393248 | tf_op jit(solution)/shard_map/ppermute | solution.py:24
  24.1 0.0 copy-done.5
  24.1 0.0 copy-start.3
  24.1 0.6 %raise.3 = bf16[768,256]{1,0:T(8,128)(2,1)S(1)} custom-call(f32[2,4,4]{2,1,0:T(4,128)S(1)} %copy-done.5, bf16[768,256]{1,0:T(8,128)(2,1)S(1)} %shard_map.55.refs_2_.own, bf16[768,256]{1,0:T(8,128)(2,1)S(1)} %collective-permute-done.2.partner.refs_7_), custom_call_target="tpu_custom_call" | custom-call | flops 589824 | bytes 1179648 | tf_op jit(solution)/shard_map/raise/pallas_call | solution.py:208
  24.8 0.0 copy-start.1
  24.8 0.0 copy-start.6
  24.8 2.8 %collective-permute-start.5 = (bf16[768,256]{1,0:T(8,128)(2,1)S(1)}, bf16[768,256]{1,0:T(8,128)(2,1)S(1)}, u32[]{:S(2)}, u32[]{:S(2)}) collective-permute-start(bf16[768,256]{1,0:T(8,128)(2,1)S(1)} %raise.3), channel_id=1, source_target_pairs={{1,4},{5,8},{9,12},{13,16},{17,20},{21,24},{25,28},{29,32},{33,36}... | collective-permute-start | bytes 1179656 | tf_op jit(solution)/shard_map/ppermute | solution.py:24
  27.6 4.9 %collective-permute-done.3.partner.refs_8_ = bf16[768,256]{1,0:T(8,128)(2,1)S(1)} collective-permute-done((bf16[768,256]{1,0:T(8,128)(2,1)S(1)}, bf16[768,256]{1,0:T(8,128)(2,1)S(1)}, u32[]{:S(2)}, u32[]{:S(2)}) %collective-permute-start.3) | collective-permute-done | bytes 393248 | tf_op jit(solution)/shard_map/ppermute | solution.py:24
  32.5 0.6 %raise.4 = bf16[768,256]{1,0:T(8,128)(2,1)S(1)} custom-call(f32[2,4,4]{2,1,0:T(4,128)S(1)} %copy-done.5, bf16[768,256]{1,0:T(8,128)(2,1)S(1)} %get-tuple-element.11.own, bf16[768,256]{1,0:T(8,128)(2,1)S(1)} %collective-permute-done.3.partner.refs_8_), custom_call_target="tpu_custom_call" | custom-call | flops 589824 | bytes 1179648 | tf_op jit(solution)/shard_map/raise/pallas_call | solution.py:208
  33.2 2.7 %collective-permute-start.6 = (bf16[768,256]{1,0:T(8,128)(2,1)S(1)}, bf16[768,256]{1,0:T(8,128)(2,1)S(1)}, u32[]{:S(2)}, u32[]{:S(2)}) collective-permute-start(bf16[768,256]{1,0:T(8,128)(2,1)S(1)} %raise.4), channel_id=1, source_target_pairs={{1,4},{5,8},{9,12},{13,16},{17,20},{21,24},{25,28},{29,32},{33,36}... | collective-permute-start | bytes 1179656 | tf_op jit(solution)/shard_map/ppermute | solution.py:24
  35.9 5.1 %collective-permute-done.4.refs_9_.partner = bf16[768,256]{1,0:T(8,128)(2,1)S(1)} collective-permute-done((bf16[768,256]{1,0:T(8,128)(2,1)S(1)}, bf16[768,256]{1,0:T(8,128)(2,1)S(1)}, u32[]{:S(2)}, u32[]{:S(2)}) %collective-permute-start.4) | collective-permute-done | bytes 393248 | tf_op jit(solution)/shard_map/ppermute | solution.py:24
  41.0 0.6 %raise.5 = bf16[768,256]{1,0:T(8,128)(2,1)S(1)} custom-call(f32[2,4,4]{2,1,0:T(4,128)S(1)} %copy-done.5, bf16[768,256]{1,0:T(8,128)(2,1)S(1)} %get-tuple-element.12.own, bf16[768,256]{1,0:T(8,128)(2,1)S(1)} %collective-permute-done.4.refs_9_.partner), custom_call_target="tpu_custom_call" | custom-call | flops 589824 | bytes 1179648 | tf_op jit(solution)/shard_map/raise/pallas_call | solution.py:208
  41.6 2.0 %collective-permute-start.7 = (bf16[768,256]{1,0:T(8,128)(2,1)S(1)}, bf16[768,256]{1,0:T(8,128)(2,1)S(1)}, u32[]{:S(2)}, u32[]{:S(2)}) collective-permute-start(bf16[768,256]{1,0:T(8,128)(2,1)S(1)} %raise.5), channel_id=1, source_target_pairs={{1,4},{5,8},{9,12},{13,16},{17,20},{21,24},{25,28},{29,32},{33,36}... | collective-permute-start | bytes 1179656 | tf_op jit(solution)/shard_map/ppermute | solution.py:24
  43.6 0.0 collective-permute-done.5.refs_10_
  43.6 6.3 %collective-permute-done.6.refs_11_ = bf16[768,256]{1,0:T(8,128)(2,1)S(1)} collective-permute-done((bf16[768,256]{1,0:T(8,128)(2,1)S(1)}, bf16[768,256]{1,0:T(8,128)(2,1)S(1)}, u32[]{:S(2)}, u32[]{:S(2)}) %collective-permute-start.6) | collective-permute-done | bytes 393248 | tf_op jit(solution)/shard_map/ppermute | solution.py:24
  50.0 0.0 collective-permute-done.refs_5_
  50.0 0.0 collective-permute-done.1.refs_6_.refs_5_
  50.0 0.0 copy-done.4
  50.0 0.0 copy-done.3
  50.0 0.0 copy-done.1
  50.0 0.0 copy-done.6
  50.0 5.0 %kept.1.refs_2_ = f32[768,768]{1,0:T(8,128)S(1)} custom-call(f32[2,4,4]{2,1,0:T(4,128)S(1)} %copy-done.5, s32[64]{0:T(128)S(1)} %copy-done.6, bf16[1,1,768,768]{3,2,1,0:T(8,128)(2,1)S(1)} %copy-done.3, bf16[2,1,768,768]{3,2,1,0:T(8,128)(2,1)S(1)} %copy-done.4, bf16[2,1,768,768]{3,2,1,0:T(8,128)(2,1)S(1)} %copy-done.1, ...), custom_call_target="tpu_custom_call" | custom-call | flops 3623878656 | bytes 10616832 | tf_op jit(solution)/shard_map/kept/pallas_call | solution.py:241
  55.0 3.4 %collective-permute-done.7.refs_6_ = bf16[768,256]{1,0:T(8,128)(2,1)S(1)} collective-permute-done((bf16[768,256]{1,0:T(8,128)(2,1)S(1)}, bf16[768,256]{1,0:T(8,128)(2,1)S(1)}, u32[]{:S(2)}, u32[]{:S(2)}) %collective-permute-start.7) | collective-permute-done | bytes 393248 | tf_op jit(solution)/shard_map/ppermute | solution.py:24
  58.4 2.6 %moved.1 = bf16[1,1,768,768]{3,2,1,0:T(8,128)(2,1)} custom-call(f32[2,4,4]{2,1,0:T(4,128)S(1)} %copy-done.5, s32[64]{0:T(128)S(1)} %copy-done.6, f32[768,768]{1,0:T(8,128)S(1)} %kept.1.refs_2_, bf16[2,1,768,768]{3,2,1,0:T(8,128)(2,1)S(1)} %copy-done.4, bf16[2,1,768,768]{3,2,1,0:T(8,128)(2,1)S(1)} %copy-done.1, ...), custom_call_target="tpu_custom_call" | custom-call | flops 603979776 | bytes 5898240 | tf_op jit(solution)/shard_map/moved/pallas_call | solution.py:257
  (1 shorter events, 0.0 us)
Async XLA Ops:
  0.0 1.3 %copy-start.2 = (bf16[1,1,768,768]{3,2,1,0:T(8,128)(2,1)S(1)}, bf16[1,1,768,768]{3,2,1,0:T(8,128)(2,1)}, u32[]{:S(2)}) copy-start(bf16[1,1,768,768]{3,2,1,0:T(8,128)(2,1)} %refs_2_.1) | copy-start | bytes 3538948
  1.3 1.7 %copy-start = (bf16[2,1,768,768]{3,2,1,0:T(8,128)(2,1)S(1)}, bf16[2,1,768,768]{3,2,1,0:T(8,128)(2,1)}, u32[]{:S(2)}) copy-start(bf16[2,1,768,768]{3,2,1,0:T(8,128)(2,1)} %refs_4_.3) | copy-start | bytes 7077892
  3.0 21.1 %copy-start.5 = (f32[2,4,4]{2,1,0:T(4,128)S(1)}, f32[2,4,4]{2,1,0:T(4,128)}, u32[]{:S(2)}) copy-start(f32[2,4,4]{2,1,0:T(4,128)} %refs_0_.7) | copy-start | bytes 388
  3.0 47.0 %copy-start.4 = (bf16[2,1,768,768]{3,2,1,0:T(8,128)(2,1)S(1)}, bf16[2,1,768,768]{3,2,1,0:T(8,128)(2,1)}, u32[]{:S(2)}) copy-start(bf16[2,1,768,768]{3,2,1,0:T(8,128)(2,1)} %refs_3_.3) | copy-start | bytes 7077892
  3.6 46.4 %collective-permute-start = (bf16[768,768]{1,0:T(8,128)(2,1)S(1)}, bf16[768,768]{1,0:T(8,128)(2,1)S(1)}, u32[]{:S(2)}, u32[]{:S(2)}) collective-permute-start(bf16[768,768]{1,0:T(8,128)(2,1)S(1)} %get-tuple-element.9), channel_id=1, source_target_pairs={{5,1},{9,5},{13,9},{17,13},{21,17},{25,21},{29,25},{33,29},{37,33}... | collective-permute-start | bytes 3538952 | tf_op jit(solution)/shard_map/ppermute | solution.py:24
  4.4 45.5 %collective-permute-start.1 = (bf16[768,768]{1,0:T(8,128)(2,1)S(1)}, bf16[768,768]{1,0:T(8,128)(2,1)S(1)}, u32[]{:S(2)}, u32[]{:S(2)}) collective-permute-start(bf16[768,768]{1,0:T(8,128)(2,1)S(1)} %get-tuple-element.10), channel_id=1, source_target_pairs={{5,1},{9,5},{13,9},{17,13},{21,17},{25,21},{29,25},{33,29},{37,33}... | collective-permute-start | bytes 3538952 | tf_op jit(solution)/shard_map/ppermute | solution.py:24
  5.2 18.9 %collective-permute-start.2 = (bf16[768,256]{1,0:T(8,128)(2,1)S(1)}, bf16[768,256]{1,0:T(8,128)(2,1)S(1)}, u32[]{:S(2)}, u32[]{:S(2)}) collective-permute-start(bf16[768,256]{1,0:T(8,128)(2,1)S(1)} %shard_map.55.refs_2_.own), channel_id=1, source_target_pairs={{1,2},{5,6},{9,10},{13,14},{17,18},{21,22},{25,26},{29,30},{33,34}... | collective-permute-start | bytes 1179656 | tf_op jit(solution)/shard_map/ppermute | solution.py:24
  6.5 26.1 %collective-permute-start.3 = (bf16[768,256]{1,0:T(8,128)(2,1)S(1)}, bf16[768,256]{1,0:T(8,128)(2,1)S(1)}, u32[]{:S(2)}, u32[]{:S(2)}) collective-permute-start(bf16[768,256]{1,0:T(8,128)(2,1)S(1)} %get-tuple-element.11.own), channel_id=1, source_target_pairs={{1,2},{5,6},{9,10},{13,14},{17,18},{21,22},{25,26},{29,30},{33,34}... | collective-permute-start | bytes 1179656 | tf_op jit(solution)/shard_map/ppermute | solution.py:24
  7.8 33.2 %collective-permute-start.4 = (bf16[768,256]{1,0:T(8,128)(2,1)S(1)}, bf16[768,256]{1,0:T(8,128)(2,1)S(1)}, u32[]{:S(2)}, u32[]{:S(2)}) collective-permute-start(bf16[768,256]{1,0:T(8,128)(2,1)S(1)} %get-tuple-element.12.own), channel_id=1, source_target_pairs={{1,2},{5,6},{9,10},{13,14},{17,18},{21,22},{25,26},{29,30},{33,34}... | collective-permute-start | bytes 1179656 | tf_op jit(solution)/shard_map/ppermute | solution.py:24
  24.1 25.9 %copy-start.3 = (bf16[1,1,768,768]{3,2,1,0:T(8,128)(2,1)S(1)}, bf16[1,1,768,768]{3,2,1,0:T(8,128)(2,1)}, u32[]{:S(2)}) copy-start(bf16[1,1,768,768]{3,2,1,0:T(8,128)(2,1)} %refs_2_.1) | copy-start | bytes 3538948
  24.8 25.2 %copy-start.1 = (bf16[2,1,768,768]{3,2,1,0:T(8,128)(2,1)S(1)}, bf16[2,1,768,768]{3,2,1,0:T(8,128)(2,1)}, u32[]{:S(2)}) copy-start(bf16[2,1,768,768]{3,2,1,0:T(8,128)(2,1)} %refs_4_.3) | copy-start | bytes 7077892
  24.8 25.2 %copy-start.6 = (s32[64]{0:T(128)S(1)}, s32[64]{0:T(128)}, u32[]{:S(2)}) copy-start(s32[64]{0:T(128)} %refs_1_.5) | copy-start | bytes 772
  24.8 18.8 %collective-permute-start.5 = (bf16[768,256]{1,0:T(8,128)(2,1)S(1)}, bf16[768,256]{1,0:T(8,128)(2,1)S(1)}, u32[]{:S(2)}, u32[]{:S(2)}) collective-permute-start(bf16[768,256]{1,0:T(8,128)(2,1)S(1)} %raise.3), channel_id=1, source_target_pairs={{1,4},{5,8},{9,12},{13,16},{17,20},{21,24},{25,28},{29,32},{33,36}... | collective-permute-start | bytes 1179656 | tf_op jit(solution)/shard_map/ppermute | solution.py:24
  33.2 16.8 %collective-permute-start.6 = (bf16[768,256]{1,0:T(8,128)(2,1)S(1)}, bf16[768,256]{1,0:T(8,128)(2,1)S(1)}, u32[]{:S(2)}, u32[]{:S(2)}) collective-permute-start(bf16[768,256]{1,0:T(8,128)(2,1)S(1)} %raise.4), channel_id=1, source_target_pairs={{1,4},{5,8},{9,12},{13,16},{17,20},{21,24},{25,28},{29,32},{33,36}... | collective-permute-start | bytes 1179656 | tf_op jit(solution)/shard_map/ppermute | solution.py:24
  41.6 16.8 %collective-permute-start.7 = (bf16[768,256]{1,0:T(8,128)(2,1)S(1)}, bf16[768,256]{1,0:T(8,128)(2,1)S(1)}, u32[]{:S(2)}, u32[]{:S(2)}) collective-permute-start(bf16[768,256]{1,0:T(8,128)(2,1)S(1)} %raise.5), channel_id=1, source_target_pairs={{1,4},{5,8},{9,12},{13,16},{17,20},{21,24},{25,28},{29,32},{33,36}... | collective-permute-start | bytes 1179656 | tf_op jit(solution)/shard_map/ppermute | solution.py:24
